TPU v7x, 32 devices: a whole 2x2x4 slice. The times are simulated.
32 devices in a mesh: hst: 8 (over y, x, core), local: 4 (over z).
Axes of the slice: x: 2, y: 2, z: 4, core: 2. Of those that a mesh axis runs over, the one named last changes fastest.
Arguments:
- image_feats: bfloat16 [4096, 1152], P(('hst', 'local')), may hold values from -6 to 6
- text_feats: bfloat16 [4096, 1152], P(('hst', 'local')), may hold values from -6 to 6
- image_proj: bfloat16 [1152, 1152], replicated, may hold values from -0.1875 to 0.1875
- text_proj: bfloat16 [1152, 1152], replicated, may hold values from -0.1875 to 0.1875
- scale: float32 [1], replicated, may hold values from 4 to 16
- bias: float32 [1], replicated, may hold values from -4 to -2
Outputs:
- image_grad: float32 [4096, 1152], P(('hst', 'local'))
- text_grad: float32 [4096, 1152], P(('hst', 'local'))
All inputs are finite; a program needn't handle non-finite values.
Results may differ from a plain program's by a relative error of at most 0.005.
Values may be sent and summed in bfloat16 or wider, within the bound.
A program may use at most 64 MiB of HBM per device.

v0:
```python
import jax
import jax.numpy as jnp
from jax import lax
from jax.sharding import PartitionSpec as P

GROUP_DEVS = 8


def passed_along(value, axis, by):
    count = lax.axis_size(axis)
    return lax.ppermute(value, axis, [(i, (i + by) % count) for i in range(count)])


def project(feats, proj):
    raw_embed = jnp.dot(feats, proj, preferred_element_type=jnp.float32)
    recip = lax.rsqrt(jnp.sum(raw_embed * raw_embed, axis=1, keepdims=True) + 1e-06)
    unit = raw_embed * recip
    return (unit, recip, unit.astype(jnp.bfloat16))


def descend(unit, recip, grad_unit, proj):
    inner = jnp.sum(unit * grad_unit, axis=1, keepdims=True)
    grad_raw = (recip * (grad_unit - unit * inner)).astype(jnp.bfloat16)
    return jnp.dot(grad_raw, proj.T, preferred_element_type=jnp.float32)


def on_device(image_feats, text_feats, image_proj, text_proj, scale, bias):
    image_unit, image_recip, image_emb = project(image_feats, image_proj)
    text_unit, text_recip, text_emb = project(text_feats, text_proj)
    row_count = image_feats.shape[0]
    feat_width = text_emb.shape[1]
    dev_count = lax.axis_size("hst") * lax.axis_size("local")
    stride = dev_count // GROUP_DEVS
    position = lax.axis_index("hst") * lax.axis_size("local") + lax.axis_index("local")
    member = position // stride
    temper = scale[0]
    offset = bias[0]
    diagonal = jnp.eye(row_count, dtype=jnp.float32)

    def grad_tile(image_rows, text_rows, anchor):
        logits = (
            temper * jnp.dot(image_rows, text_rows.T, preferred_element_type=jnp.float32) + offset
        )
        matched = jnp.where(anchor == member, diagonal, jnp.zeros_like(diagonal))
        return (jax.nn.sigmoid(logits) - matched).astype(jnp.bfloat16)

    image_block = image_emb
    text_block = text_emb
    image_sum = jnp.zeros((row_count, feat_width), jnp.float32)
    text_sum = jnp.zeros((row_count, feat_width), jnp.float32)
    for turn_idx in range(GROUP_DEVS):
        anchor = (member - turn_idx) % GROUP_DEVS
        own_images = grad_tile(image_emb, text_block, anchor)
        image_sum = image_sum + jnp.dot(own_images, text_block, preferred_element_type=jnp.float32)
        own_texts = grad_tile(image_block, text_emb, anchor)
        text_sum = text_sum + jnp.einsum(
            "mq,me->qe", own_texts, image_block, preferred_element_type=jnp.float32
        )
        if turn_idx + 1 < GROUP_DEVS:
            image_block, text_block = passed_along(
                (image_block, text_block), ("hst", "local"), stride
            )
    image_grad = descend(image_unit, image_recip, temper * image_sum, image_proj)
    text_grad = descend(text_unit, text_recip, temper * text_sum, text_proj)
    return (image_grad, text_grad)


def solution(mesh):
    in_specs = (P(("hst", "local"), None), P(("hst", "local"), None), P(), P(), P(), P())
    out_specs = (P(("hst", "local"), None), P(("hst", "local"), None))
    return jax.shard_map(
        on_device, mesh=mesh, in_specs=in_specs, out_specs=out_specs, check_vma=False
    )
```

profile of v0, /device:TPU:0, one launch (start us, length us, event | category | flops | bytes accessed | tf_op | source)
XLA Modules:
  0.0 71.8 jit_solution(13789425007882733545)
XLA Ops:
  0.6 0.0 copy-start
  0.6 0.0 copy-start.3
  0.7 2.7 %multiply_reduce_fusion.3 = (f32[128]{0:T(128)S(1)}, f32[128,1152]{1,0:T(8,128)S(1)}) fusion(bf16[128,1152]{1,0:T(8,128)(2,1)} %param.6, bf16[1152,1152]{1,0:T(8,128)(2,1)} %param.8), kind=kOutput, calls=%fused_computation.141 | convolution fusion | flops 340033408 | bytes 3539456 | tf_op jit(solution)/shard_map/dot_general | solution.py:15
  3.3 0.0 copy-start.1
  3.4 0.1 multiply_convert_fusion.3
  3.5 0.5 collective-permute-start.7
  4.0 0.0 copy-done
  4.0 0.0 copy-done.3
  4.0 0.7 multiply_reduce_fusion.2
  4.7 0.0 copy-start.2
  4.7 0.1 multiply_convert_fusion.2
  4.9 0.0 copy-done.1
  4.9 2.6 %collective-permute-start = (bf16[128,1152]{1,0:T(8,128)(2,1)S(1)}, bf16[128,1152]{1,0:T(8,128)(2,1)}, u32[]{:S(2)}, u32[]{:S(2)}) collective-permute-start(bf16[128,1152]{1,0:T(8,128)(2,1)S(1)} %multiply_convert_fusion.2), channel_id=1, source_target_pairs={{0,4},{1,5},{2,6},{3,7},{4,8},{5,9},{6,10},{7,11},{8,12},{9,13},{1... | collective-permute-start | bytes 884744 | tf_op jit(solution)/shard_map/ppermute | solution.py:11
  7.5 0.0 copy-done.2
  8.8 0.3 fusion.92
  9.1 0.0 copy-start.4
  9.1 0.6 copy-done.4
  9.7 1.1 %fusion.212 = f32[128,1152]{1,0:T(8,128)} fusion(bf16[128,128]{1,0:T(8,128)(2,1)S(1)} %fusion.92, bf16[128,1152]{1,0:T(8,128)(2,1)S(1)} %multiply_convert_fusion.3), kind=kOutput, calls=%fused_computation.260 | convolution fusion | flops 37748736 | bytes 917504 | tf_op jit(solution)/shard_map/mq,me->qe/dot_general | solution.py:56
  10.7 1.8 %fusion.211 = f32[128,1152]{1,0:T(8,128)} fusion(bf16[128,128]{1,0:T(8,128)(2,1)} %copy-done.4, bf16[128,1152]{1,0:T(8,128)(2,1)S(1)} %multiply_convert_fusion.2), kind=kOutput, calls=%fused_computation.259 | convolution fusion | flops 37748736 | bytes 917504 | tf_op jit(solution)/shard_map/dot_general | solution.py:54
  12.5 0.0 collective-permute-done.7
  12.5 0.6 collective-permute-start.8
  13.2 1.4 %collective-permute-done = bf16[128,1152]{1,0:T(8,128)(2,1)} collective-permute-done((bf16[128,1152]{1,0:T(8,128)(2,1)S(1)}, bf16[128,1152]{1,0:T(8,128)(2,1)}, u32[]{:S(2)}, u32[]{:S(2)}) %collective-permute-start) | collective-permute-done | bytes 294944 | tf_op jit(solution)/shard_map/ppermute | solution.py:11
  14.6 0.0 collective-permute-start.1
  14.6 2.5 %convolution_add_fusion.6 = f32[128,1152]{1,0:T(8,128)} fusion(f32[128,1152]{1,0:T(8,128)} %fusion.212, bf16[128,1152]{1,0:T(8,128)(2,1)S(1)} %collective-permute-done.7, bf16[128,1152]{1,0:T(8,128)(2,1)S(1)} %multiply_convert_fusion.2, f32[]{:T(128)} %bitcast.78, f32[]{:T(128)} %bitcast.64, pred[]{:T(512)S(6)} %eq.60), kind=kOutput, calls=%fused_computation.7 | convolution fusion | flops 75808768 | bytes 1769481 | tf_op jit(solution)/shard_map/mq,me->qe/dot_general | solution.py:56
  17.0 2.6 %convolution_add_fusion.13 = f32[128,1152]{1,0:T(8,128)} fusion(f32[128,1152]{1,0:T(8,128)} %fusion.211, bf16[128,1152]{1,0:T(8,128)(2,1)} %collective-permute-done, bf16[128,1152]{1,0:T(8,128)(2,1)S(1)} %multiply_convert_fusion.3, f32[]{:T(128)} %bitcast.85, f32[]{:T(128)} %bitcast.70, pred[]{:T(512)S(6)} %eq.60), kind=kOutput, calls=%fused_computation.15 | convolution fusion | flops 75808768 | bytes 1769481 | tf_op jit(solution)/shard_map/dot_general | solution.py:54
  19.7 0.0 collective-permute-done.8
  19.7 1.4 %collective-permute-start.9 = (bf16[128,1152]{1,0:T(8,128)(2,1)}, bf16[128,1152]{1,0:T(8,128)(2,1)S(1)}, u32[]{:S(2)}, u32[]{:S(2)}) collective-permute-start(bf16[128,1152]{1,0:T(8,128)(2,1)} %collective-permute-done.8), channel_id=1, source_target_pairs={{0,4},{1,5},{2,6},{3,7},{4,8},{5,9},{6,10},{7,11},{8,12},{9,13},{1... | collective-permute-start | bytes 884744 | tf_op jit(solution)/shard_map/ppermute | solution.py:11
  21.1 1.7 %collective-permute-done.1 = bf16[128,1152]{1,0:T(8,128)(2,1)} collective-permute-done((bf16[128,1152]{1,0:T(8,128)(2,1)}, bf16[128,1152]{1,0:T(8,128)(2,1)}, u32[]{:S(2)}, u32[]{:S(2)}) %collective-permute-start.1) | collective-permute-done | bytes 294944 | tf_op jit(solution)/shard_map/ppermute | solution.py:11
  22.9 0.0 collective-permute-start.2
  22.9 2.7 %convolution_add_fusion.5 = f32[128,1152]{1,0:T(8,128)} fusion(f32[128,1152]{1,0:T(8,128)} %convolution_add_fusion.6, bf16[128,1152]{1,0:T(8,128)(2,1)} %collective-permute-done.8, bf16[128,1152]{1,0:T(8,128)(2,1)S(1)} %multiply_convert_fusion.2, f32[]{:T(128)} %bitcast.77, f32[]{:T(128)} %bitcast.63, pred[]{:T(512)S(6)} %eq.61), kind=kOutput, calls=%fused_computation.6 | convolution fusion | flops 75808768 | bytes 1769481 | tf_op jit(solution)/shard_map/mq,me->qe/dot_general | solution.py:56
  25.5 2.6 %convolution_add_fusion.12 = f32[128,1152]{1,0:T(8,128)} fusion(f32[128,1152]{1,0:T(8,128)} %convolution_add_fusion.13, bf16[128,1152]{1,0:T(8,128)(2,1)} %collective-permute-done.1, bf16[128,1152]{1,0:T(8,128)(2,1)S(1)} %multiply_convert_fusion.3, f32[]{:T(128)} %bitcast.84, f32[]{:T(128)} %bitcast.69, pred[]{:T(512)S(6)} %eq.61), kind=kOutput, calls=%fused_computation.14 | convolution fusion | flops 75808768 | bytes 1769481 | tf_op jit(solution)/shard_map/dot_general | solution.py:54
  28.1 0.0 collective-permute-done.9
  28.1 0.8 %collective-permute-start.10 = (bf16[128,1152]{1,0:T(8,128)(2,1)S(1)}, bf16[128,1152]{1,0:T(8,128)(2,1)}, u32[]{:S(2)}, u32[]{:S(2)}) collective-permute-start(bf16[128,1152]{1,0:T(8,128)(2,1)S(1)} %collective-permute-done.9), channel_id=1, source_target_pairs={{0,4},{1,5},{2,6},{3,7},{4,8},{5,9},{6,10},{7,11},{8,12},{9,13},{1... | collective-permute-start | bytes 884744 | tf_op jit(solution)/shard_map/ppermute | solution.py:11
  28.9 1.3 %collective-permute-done.2 = bf16[128,1152]{1,0:T(8,128)(2,1)} collective-permute-done((bf16[128,1152]{1,0:T(8,128)(2,1)}, bf16[128,1152]{1,0:T(8,128)(2,1)}, u32[]{:S(2)}, u32[]{:S(2)}) %collective-permute-start.2) | collective-permute-done | bytes 294944 | tf_op jit(solution)/shard_map/ppermute | solution.py:11
  30.2 0.0 collective-permute-start.3
  30.2 2.5 %convolution_add_fusion.4 = f32[128,1152]{1,0:T(8,128)} fusion(f32[128,1152]{1,0:T(8,128)} %convolution_add_fusion.5, bf16[128,1152]{1,0:T(8,128)(2,1)S(1)} %collective-permute-done.9, bf16[128,1152]{1,0:T(8,128)(2,1)S(1)} %multiply_convert_fusion.2, f32[]{:T(128)} %bitcast.76, f32[]{:T(128)} %bitcast.62, pred[]{:T(512)S(6)} %eq.62), kind=kOutput, calls=%fused_computation.5 | convolution fusion | flops 75808768 | bytes 1769481 | tf_op jit(solution)/shard_map/mq,me->qe/dot_general | solution.py:56
  32.7 2.6 %convolution_add_fusion.11 = f32[128,1152]{1,0:T(8,128)} fusion(f32[128,1152]{1,0:T(8,128)} %convolution_add_fusion.12, bf16[128,1152]{1,0:T(8,128)(2,1)} %collective-permute-done.2, bf16[128,1152]{1,0:T(8,128)(2,1)S(1)} %multiply_convert_fusion.3, f32[]{:T(128)} %bitcast.83, f32[]{:T(128)} %bitcast.68, pred[]{:T(512)S(6)} %eq.62), kind=kOutput, calls=%fused_computation.13 | convolution fusion | flops 75808768 | bytes 1769481 | tf_op jit(solution)/shard_map/dot_general | solution.py:54
  35.3 0.0 collective-permute-done.10
  35.3 1.1 %collective-permute-start.11 = (bf16[128,1152]{1,0:T(8,128)(2,1)}, bf16[128,1152]{1,0:T(8,128)(2,1)}, u32[]{:S(2)}, u32[]{:S(2)}) collective-permute-start(bf16[128,1152]{1,0:T(8,128)(2,1)} %collective-permute-done.10), channel_id=1, source_target_pairs={{0,4},{1,5},{2,6},{3,7},{4,8},{5,9},{6,10},{7,11},{8,12},{9,13},{1... | collective-permute-start | bytes 884744 | tf_op jit(solution)/shard_map/ppermute | solution.py:11
  36.5 2.0 %collective-permute-done.3 = bf16[128,1152]{1,0:T(8,128)(2,1)} collective-permute-done((bf16[128,1152]{1,0:T(8,128)(2,1)}, bf16[128,1152]{1,0:T(8,128)(2,1)}, u32[]{:S(2)}, u32[]{:S(2)}) %collective-permute-start.3) | collective-permute-done | bytes 294944 | tf_op jit(solution)/shard_map/ppermute | solution.py:11
  38.5 0.0 collective-permute-start.4
  38.5 2.7 %convolution_add_fusion.3 = f32[128,1152]{1,0:T(8,128)} fusion(f32[128,1152]{1,0:T(8,128)} %convolution_add_fusion.4, bf16[128,1152]{1,0:T(8,128)(2,1)} %collective-permute-done.10, bf16[128,1152]{1,0:T(8,128)(2,1)S(1)} %multiply_convert_fusion.2, f32[]{:T(128)} %bitcast.75, f32[]{:T(128)} %bitcast.61, pred[]{:T(512)S(6)} %eq.63), kind=kOutput, calls=%fused_computation.4 | convolution fusion | flops 75808768 | bytes 1769481 | tf_op jit(solution)/shard_map/mq,me->qe/dot_general | solution.py:56
  41.1 2.6 %convolution_add_fusion.10 = f32[128,1152]{1,0:T(8,128)} fusion(f32[128,1152]{1,0:T(8,128)} %convolution_add_fusion.11, bf16[128,1152]{1,0:T(8,128)(2,1)} %collective-permute-done.3, bf16[128,1152]{1,0:T(8,128)(2,1)S(1)} %multiply_convert_fusion.3, f32[]{:T(128)} %bitcast.82, f32[]{:T(128)} %bitcast.67, pred[]{:T(512)S(6)} %eq.63), kind=kOutput, calls=%fused_computation.12 | convolution fusion | flops 75808768 | bytes 1769481 | tf_op jit(solution)/shard_map/dot_general | solution.py:54
  43.7 0.0 collective-permute-done.11
  43.7 0.8 %collective-permute-start.12 = (bf16[128,1152]{1,0:T(8,128)(2,1)}, bf16[128,1152]{1,0:T(8,128)(2,1)}, u32[]{:S(2)}, u32[]{:S(2)}) collective-permute-start(bf16[128,1152]{1,0:T(8,128)(2,1)} %collective-permute-done.11), channel_id=1, source_target_pairs={{0,4},{1,5},{2,6},{3,7},{4,8},{5,9},{6,10},{7,11},{8,12},{9,13},{1... | collective-permute-start | bytes 884744 | tf_op jit(solution)/shard_map/ppermute | solution.py:11
  44.5 1.3 %collective-permute-done.4 = bf16[128,1152]{1,0:T(8,128)(2,1)} collective-permute-done((bf16[128,1152]{1,0:T(8,128)(2,1)}, bf16[128,1152]{1,0:T(8,128)(2,1)}, u32[]{:S(2)}, u32[]{:S(2)}) %collective-permute-start.4) | collective-permute-done | bytes 294944 | tf_op jit(solution)/shard_map/ppermute | solution.py:11
  45.8 0.0 collective-permute-start.5
  45.8 2.7 %convolution_add_fusion.2 = f32[128,1152]{1,0:T(8,128)} fusion(f32[128,1152]{1,0:T(8,128)} %convolution_add_fusion.3, bf16[128,1152]{1,0:T(8,128)(2,1)} %collective-permute-done.11, bf16[128,1152]{1,0:T(8,128)(2,1)S(1)} %multiply_convert_fusion.2, f32[]{:T(128)} %bitcast.74, f32[]{:T(128)} %bitcast.60, pred[]{:T(512)S(6)} %eq.64), kind=kOutput, calls=%fused_computation.3 | convolution fusion | flops 75808768 | bytes 1769481 | tf_op jit(solution)/shard_map/mq,me->qe/dot_general | solution.py:56
  48.5 2.6 %convolution_add_fusion.9 = f32[128,1152]{1,0:T(8,128)} fusion(f32[128,1152]{1,0:T(8,128)} %convolution_add_fusion.10, bf16[128,1152]{1,0:T(8,128)(2,1)} %collective-permute-done.4, bf16[128,1152]{1,0:T(8,128)(2,1)S(1)} %multiply_convert_fusion.3, f32[]{:T(128)} %bitcast.81, f32[]{:T(128)} %bitcast.66, pred[]{:T(512)S(6)} %eq.64), kind=kOutput, calls=%fused_computation.11 | convolution fusion | flops 75808768 | bytes 1769481 | tf_op jit(solution)/shard_map/dot_general | solution.py:54
  51.1 0.0 collective-permute-done.12
  51.1 1.1 %collective-permute-start.13 = (bf16[128,1152]{1,0:T(8,128)(2,1)}, bf16[128,1152]{1,0:T(8,128)(2,1)}, u32[]{:S(2)}, u32[]{:S(2)}) collective-permute-start(bf16[128,1152]{1,0:T(8,128)(2,1)} %collective-permute-done.12), channel_id=1, source_target_pairs={{0,4},{1,5},{2,6},{3,7},{4,8},{5,9},{6,10},{7,11},{8,12},{9,13},{1... | collective-permute-start | bytes 884744 | tf_op jit(solution)/shard_map/ppermute | solution.py:11
  52.2 1.9 %collective-permute-done.5 = bf16[128,1152]{1,0:T(8,128)(2,1)S(1)} collective-permute-done((bf16[128,1152]{1,0:T(8,128)(2,1)}, bf16[128,1152]{1,0:T(8,128)(2,1)S(1)}, u32[]{:S(2)}, u32[]{:S(2)}) %collective-permute-start.5) | collective-permute-done | bytes 294944 | tf_op jit(solution)/shard_map/ppermute | solution.py:11
  54.2 0.0 collective-permute-start.6
  54.2 2.7 %convolution_add_fusion.1 = f32[128,1152]{1,0:T(8,128)} fusion(f32[128,1152]{1,0:T(8,128)} %convolution_add_fusion.2, bf16[128,1152]{1,0:T(8,128)(2,1)} %collective-permute-done.12, bf16[128,1152]{1,0:T(8,128)(2,1)S(1)} %multiply_convert_fusion.2, f32[]{:T(128)} %bitcast.73, f32[]{:T(128)} %bitcast.59, pred[]{:T(512)S(6)} %eq.65), kind=kOutput, calls=%fused_computation.2 | convolution fusion | flops 75808768 | bytes 1769481 | tf_op jit(solution)/shard_map/mq,me->qe/dot_general | solution.py:56
  56.9 2.4 %convolution_add_fusion.8 = f32[128,1152]{1,0:T(8,128)} fusion(f32[128,1152]{1,0:T(8,128)} %convolution_add_fusion.9, bf16[128,1152]{1,0:T(8,128)(2,1)S(1)} %collective-permute-done.5, bf16[128,1152]{1,0:T(8,128)(2,1)S(1)} %multiply_convert_fusion.3, f32[]{:T(128)} %bitcast.80, f32[]{:T(128)} %bitcast.65, pred[]{:T(512)S(6)} %eq.65), kind=kOutput, calls=%fused_computation.10 | convolution fusion | flops 75808768 | bytes 1769481 | tf_op jit(solution)/shard_map/dot_general | solution.py:54
  59.3 0.0 collective-permute-done.13
  59.3 2.9 %multiply_reduce_fusion = (f32[128]{0:T(128)S(1)}, f32[128,1152]{1,0:T(8,128)}) fusion(f32[128,1152]{1,0:T(8,128)} %copy-done.2, f32[128]{0:T(128)S(1)} %add_rsqrt_fusion, f32[128,1152]{1,0:T(8,128)} %convolution_add_fusion.1, bf16[128,1152]{1,0:T(8,128)(2,1)} %collective-permute-done.13, bf16[128,1152]{1,0:T(8,128)(2,1)S(1)} %multiply_convert_fusion.2, ...), kind=kOutput, calls=%fused_computation.137 | convolution fusion | flops 76398464 | bytes 2360329 | tf_op jit(solution)/shard_map/mq,me->qe/dot_general | solution.py:56
  62.2 3.0 %fusion.108 = f32[128,1152]{1,0:T(8,128)} fusion(bf16[1152,1152]{1,0:T(8,128)(2,1)S(1)} %copy-done, f32[128,1152]{1,0:T(8,128)} %get-tuple-element.9, f32[128,1152]{1,0:T(8,128)} %copy-done.2, f32[128]{0:T(128)S(1)} %get-tuple-element.8, f32[128]{0:T(128)S(1)} %add_rsqrt_fusion), kind=kOutput, calls=%fused_computation.145 | convolution fusion | flops 340475904 | bytes 4424704 | tf_op jit(solution)/shard_map/dot_general | solution.py:24
  65.1 0.0 collective-permute-done.6
  65.2 2.8 %multiply_reduce_fusion.1 = (f32[128]{0:T(128)S(1)}, f32[128,1152]{1,0:T(8,128)}) fusion(f32[128,1152]{1,0:T(8,128)} %copy-done.1, f32[128]{0:T(128)S(1)} %add_rsqrt_fusion.1, f32[128,1152]{1,0:T(8,128)} %convolution_add_fusion.8, bf16[128,1152]{1,0:T(8,128)(2,1)} %collective-permute-done.6, bf16[128,1152]{1,0:T(8,128)(2,1)S(1)} %multiply_convert_fusion.3, ...), kind=kOutput, calls=%fused_computation.139 | convolution fusion | flops 76398464 | bytes 2360329 | tf_op jit(solution)/shard_map/dot_general | solution.py:54
  67.9 3.9 %fusion.107 = f32[128,1152]{1,0:T(8,128)} fusion(bf16[1152,1152]{1,0:T(8,128)(2,1)} %param.8, f32[128,1152]{1,0:T(8,128)} %get-tuple-element.7, f32[128,1152]{1,0:T(8,128)} %copy-done.1, f32[128]{0:T(128)S(1)} %get-tuple-element.6, f32[128]{0:T(128)S(1)} %add_rsqrt_fusion.1), kind=kOutput, calls=%fused_computation.144 | convolution fusion | flops 340475904 | bytes 4424704 | tf_op jit(solution)/shard_map/dot_general | solution.py:24
  (2 shorter events, 0.0 us)
Async XLA Ops:
  0.6 3.4 %copy-start = (bf16[1152,1152]{1,0:T(8,128)(2,1)S(1)}, bf16[1152,1152]{1,0:T(8,128)(2,1)}, u32[]{:S(2)}) copy-start(bf16[1152,1152]{1,0:T(8,128)(2,1)} %param.9) | copy-start | bytes 7962628
  0.6 3.4 %copy-start.3 = (bf16[128,1152]{1,0:T(8,128)(2,1)S(1)}, bf16[128,1152]{1,0:T(8,128)(2,1)}, u32[]{:S(2)}) copy-start(bf16[128,1152]{1,0:T(8,128)(2,1)} %param.7) | copy-start | bytes 884740
  3.3 1.5 %copy-start.1 = (f32[128,1152]{1,0:T(8,128)}, f32[128,1152]{1,0:T(8,128)S(1)}, u32[]{:S(2)}) copy-start(f32[128,1152]{1,0:T(8,128)S(1)} %get-tuple-element.3) | copy-start | bytes 1769476
  3.5 9.1 %collective-permute-start.7 = (bf16[128,1152]{1,0:T(8,128)(2,1)S(1)}, bf16[128,1152]{1,0:T(8,128)(2,1)S(1)}, u32[]{:S(2)}, u32[]{:S(2)}) collective-permute-start(bf16[128,1152]{1,0:T(8,128)(2,1)S(1)} %multiply_convert_fusion.3), channel_id=1, source_target_pairs={{0,4},{1,5},{2,6},{3,7},{4,8},{5,9},{6,10},{7,11},{8,12},{9,13},{1... | collective-permute-start | bytes 884744 | tf_op jit(solution)/shard_map/ppermute | solution.py:11
  4.7 2.8 %copy-start.2 = (f32[128,1152]{1,0:T(8,128)}, f32[128,1152]{1,0:T(8,128)S(1)}, u32[]{:S(2)}) copy-start(f32[128,1152]{1,0:T(8,128)S(1)} %get-tuple-element.5) | copy-start | bytes 1769476
  4.9 9.7 %collective-permute-start = (bf16[128,1152]{1,0:T(8,128)(2,1)S(1)}, bf16[128,1152]{1,0:T(8,128)(2,1)}, u32[]{:S(2)}, u32[]{:S(2)}) collective-permute-start(bf16[128,1152]{1,0:T(8,128)(2,1)S(1)} %multiply_convert_fusion.2), channel_id=1, source_target_pairs={{0,4},{1,5},{2,6},{3,7},{4,8},{5,9},{6,10},{7,11},{8,12},{9,13},{1... | collective-permute-start | bytes 884744 | tf_op jit(solution)/shard_map/ppermute | solution.py:11
  9.1 0.6 copy-start.4
  12.5 7.2 %collective-permute-start.8 = (bf16[128,1152]{1,0:T(8,128)(2,1)S(1)}, bf16[128,1152]{1,0:T(8,128)(2,1)}, u32[]{:S(2)}, u32[]{:S(2)}) collective-permute-start(bf16[128,1152]{1,0:T(8,128)(2,1)S(1)} %collective-permute-done.7), channel_id=1, source_target_pairs={{0,4},{1,5},{2,6},{3,7},{4,8},{5,9},{6,10},{7,11},{8,12},{9,13},{1... | collective-permute-start | bytes 884744 | tf_op jit(solution)/shard_map/ppermute | solution.py:11
  14.6 8.3 %collective-permute-start.1 = (bf16[128,1152]{1,0:T(8,128)(2,1)}, bf16[128,1152]{1,0:T(8,128)(2,1)}, u32[]{:S(2)}, u32[]{:S(2)}) collective-permute-start(bf16[128,1152]{1,0:T(8,128)(2,1)} %collective-permute-done), channel_id=1, source_target_pairs={{0,4},{1,5},{2,6},{3,7},{4,8},{5,9},{6,10},{7,11},{8,12},{9,13},{1... | collective-permute-start | bytes 884744 | tf_op jit(solution)/shard_map/ppermute | solution.py:11
  19.7 8.4 %collective-permute-start.9 = (bf16[128,1152]{1,0:T(8,128)(2,1)}, bf16[128,1152]{1,0:T(8,128)(2,1)S(1)}, u32[]{:S(2)}, u32[]{:S(2)}) collective-permute-start(bf16[128,1152]{1,0:T(8,128)(2,1)} %collective-permute-done.8), channel_id=1, source_target_pairs={{0,4},{1,5},{2,6},{3,7},{4,8},{5,9},{6,10},{7,11},{8,12},{9,13},{1... | collective-permute-start | bytes 884744 | tf_op jit(solution)/shard_map/ppermute | solution.py:11
  22.9 7.4 %collective-permute-start.2 = (bf16[128,1152]{1,0:T(8,128)(2,1)}, bf16[128,1152]{1,0:T(8,128)(2,1)}, u32[]{:S(2)}, u32[]{:S(2)}) collective-permute-start(bf16[128,1152]{1,0:T(8,128)(2,1)} %collective-permute-done.1), channel_id=1, source_target_pairs={{0,4},{1,5},{2,6},{3,7},{4,8},{5,9},{6,10},{7,11},{8,12},{9,13},{1... | collective-permute-start | bytes 884744 | tf_op jit(solution)/shard_map/ppermute | solution.py:11
  28.1 7.2 %collective-permute-start.10 = (bf16[128,1152]{1,0:T(8,128)(2,1)S(1)}, bf16[128,1152]{1,0:T(8,128)(2,1)}, u32[]{:S(2)}, u32[]{:S(2)}) collective-permute-start(bf16[128,1152]{1,0:T(8,128)(2,1)S(1)} %collective-permute-done.9), channel_id=1, source_target_pairs={{0,4},{1,5},{2,6},{3,7},{4,8},{5,9},{6,10},{7,11},{8,12},{9,13},{1... | collective-permute-start | bytes 884744 | tf_op jit(solution)/shard_map/ppermute | solution.py:11
  30.2 8.2 %collective-permute-start.3 = (bf16[128,1152]{1,0:T(8,128)(2,1)}, bf16[128,1152]{1,0:T(8,128)(2,1)}, u32[]{:S(2)}, u32[]{:S(2)}) collective-permute-start(bf16[128,1152]{1,0:T(8,128)(2,1)} %collective-permute-done.2), channel_id=1, source_target_pairs={{0,4},{1,5},{2,6},{3,7},{4,8},{5,9},{6,10},{7,11},{8,12},{9,13},{1... | collective-permute-start | bytes 884744 | tf_op jit(solution)/shard_map/ppermute | solution.py:11
  35.3 8.4 %collective-permute-start.11 = (bf16[128,1152]{1,0:T(8,128)(2,1)}, bf16[128,1152]{1,0:T(8,128)(2,1)}, u32[]{:S(2)}, u32[]{:S(2)}) collective-permute-start(bf16[128,1152]{1,0:T(8,128)(2,1)} %collective-permute-done.10), channel_id=1, source_target_pairs={{0,4},{1,5},{2,6},{3,7},{4,8},{5,9},{6,10},{7,11},{8,12},{9,13},{1... | collective-permute-start | bytes 884744 | tf_op jit(solution)/shard_map/ppermute | solution.py:11
  38.5 7.4 %collective-permute-start.4 = (bf16[128,1152]{1,0:T(8,128)(2,1)}, bf16[128,1152]{1,0:T(8,128)(2,1)}, u32[]{:S(2)}, u32[]{:S(2)}) collective-permute-start(bf16[128,1152]{1,0:T(8,128)(2,1)} %collective-permute-done.3), channel_id=1, source_target_pairs={{0,4},{1,5},{2,6},{3,7},{4,8},{5,9},{6,10},{7,11},{8,12},{9,13},{1... | collective-permute-start | bytes 884744 | tf_op jit(solution)/shard_map/ppermute | solution.py:11
  43.7 7.4 %collective-permute-start.12 = (bf16[128,1152]{1,0:T(8,128)(2,1)}, bf16[128,1152]{1,0:T(8,128)(2,1)}, u32[]{:S(2)}, u32[]{:S(2)}) collective-permute-start(bf16[128,1152]{1,0:T(8,128)(2,1)} %collective-permute-done.11), channel_id=1, source_target_pairs={{0,4},{1,5},{2,6},{3,7},{4,8},{5,9},{6,10},{7,11},{8,12},{9,13},{1... | collective-permute-start | bytes 884744 | tf_op jit(solution)/shard_map/ppermute | solution.py:11
  45.8 8.3 %collective-permute-start.5 = (bf16[128,1152]{1,0:T(8,128)(2,1)}, bf16[128,1152]{1,0:T(8,128)(2,1)S(1)}, u32[]{:S(2)}, u32[]{:S(2)}) collective-permute-start(bf16[128,1152]{1,0:T(8,128)(2,1)} %collective-permute-done.4), channel_id=1, source_target_pairs={{0,4},{1,5},{2,6},{3,7},{4,8},{5,9},{6,10},{7,11},{8,12},{9,13},{1... | collective-permute-start | bytes 884744 | tf_op jit(solution)/shard_map/ppermute | solution.py:11
  51.1 8.2 %collective-permute-start.13 = (bf16[128,1152]{1,0:T(8,128)(2,1)}, bf16[128,1152]{1,0:T(8,128)(2,1)}, u32[]{:S(2)}, u32[]{:S(2)}) collective-permute-start(bf16[128,1152]{1,0:T(8,128)(2,1)} %collective-permute-done.12), channel_id=1, source_target_pairs={{0,4},{1,5},{2,6},{3,7},{4,8},{5,9},{6,10},{7,11},{8,12},{9,13},{1... | collective-permute-start | bytes 884744 | tf_op jit(solution)/shard_map/ppermute | solution.py:11
  54.2 11.0 %collective-permute-start.6 = (bf16[128,1152]{1,0:T(8,128)(2,1)S(1)}, bf16[128,1152]{1,0:T(8,128)(2,1)}, u32[]{:S(2)}, u32[]{:S(2)}) collective-permute-start(bf16[128,1152]{1,0:T(8,128)(2,1)S(1)} %collective-permute-done.5), channel_id=1, source_target_pairs={{0,4},{1,5},{2,6},{3,7},{4,8},{5,9},{6,10},{7,11},{8,12},{9,13},{1... | collective-permute-start | bytes 884744 | tf_op jit(solution)/shard_map/ppermute | solution.py:11
where the time goes:
time: 72.9 us; the launch traced here: 71.8 us
  matrix products  50.2 us (69%)
  waiting for transfers between devices  9.71 us (13%)
  starting transfers between devices  9.06 us (12%)
  between operations  2.05 us (3%)
    dot_general x8, matrix products, on_device(): jnp.dot(own_images, text_block, preferred_element_type=jnp.float32)  20 us
    dot_general x8, matrix products, on_device(): jnp.einsum('mq,me->qe', own_texts, image_block, preferred_element_type=jn...  19.6 us
    ppermute x14, waiting for transfers between devices, passed_along(): lax.ppermute(value, axis, [(i, (i + by) % count) for i in range(count)])  9.71 us
    ppermute x14, starting transfers between devices, passed_along(): lax.ppermute(value, axis, [(i, (i + by) % count) for i in range(count)])  9.06 us
    dot_general x2, matrix products, descend(): return jnp.dot(grad_raw, proj.T, preferred_element_type=jnp.float32)  6.86 us
    dot_general x2, matrix products, project(): raw_embed = jnp.dot(feats, proj, preferred_element_type=jnp.float32)  3.37 us
  transfers between devices with their start and end apart: 14, of which 6 were waited for; matrix products, arithmetic and copies ran while one was open for 57% of the time, Pallas kernels for 0%

commit v1 on v0

v1 whole, which is shorter than its diff:
```python
import functools

import jax
import jax.numpy as jnp
from jax import lax
from jax.experimental import pallas as pl
from jax.experimental.pallas import tpu as pltpu
from jax.sharding import PartitionSpec as P

GROUP_DEVS = 8
CHUNKS = 2
SIBLING, PARTNER, RELAY, BACK = range(4)


def flipped(member, bit):
    return member + bit - 2 * bit * lax.rem(lax.div(member, bit), 2)


def kernel(
    axis_sizes,
    image_feats,
    text_feats,
    image_proj,
    text_proj,
    scale,
    bias,
    image_grad,
    text_grad,
    feats,
    proj,
    emb,
    unit,
    recip,
    own_sum,
    away_sum,
    away_out,
    away_in,
    load_sem,
    send_sem,
    recv_sem,
):
    hosts, locals_ = axis_sizes
    stride = hosts * locals_ // GROUP_DEVS
    position = lax.axis_index("hst") * locals_ + lax.axis_index("local")
    member = lax.div(position, stride)
    rest = lax.rem(position, stride)

    def device_of(other):
        place = other * stride + rest
        return (lax.div(place, locals_), lax.rem(place, locals_))

    sibling = device_of(flipped(member, 1))
    partners = (device_of(flipped(member, 2)), device_of(flipped(member, 4)))

    rows = image_feats.shape[0]
    part = rows // CHUNKS
    temper = scale[0]
    offset = bias[0]

    feat_loads = []
    proj_loads = []
    for side, (feat_ref, proj_ref) in enumerate(
        ((image_feats, image_proj), (text_feats, text_proj))
    ):
        feat_loads.append(
            pltpu.make_async_copy(feat_ref, feats.at[side], load_sem.at[side, 0])
        )
        proj_loads.append(
            pltpu.make_async_copy(proj_ref, proj.at[side], load_sem.at[side, 1])
        )
        feat_loads[side].start()
        proj_loads[side].start()

    barrier = pltpu.get_barrier_semaphore()
    for other in (sibling,) + partners:
        pl.semaphore_signal(
            barrier, inc=1, device_id=other, device_id_type=pl.DeviceIdType.MESH
        )

    def remote(src, dst, kind, side, piece, device):
        return pltpu.make_async_remote_copy(
            src_ref=src,
            dst_ref=dst,
            send_sem=send_sem.at[kind, side, piece],
            recv_sem=recv_sem.at[kind, side, piece],
            device_id=device,
            device_id_type=pl.DeviceIdType.MESH,
        )

    copies = {}

    def send(kind, side, piece):
        span = pl.ds(piece * part, part)
        if kind == SIBLING:
            src, dst, device = emb.at[side, 0, span], emb.at[side, 1, span], sibling
        elif kind == PARTNER:
            src, dst, device = emb.at[side, 0, span], emb.at[side, 2, span], partners[side]
        elif kind == RELAY:
            src, dst, device = emb.at[side, 2, span], emb.at[side, 3, span], sibling
        else:
            src, dst, device = away_out.at[side, span], away_in.at[side, span], partners[side]
        copy = remote(src, dst, kind, side, piece, device)
        copy.start()
        copies[kind, side, piece] = copy

    for side in range(2):
        feat_loads[side].wait()
        proj_loads[side].wait()
        raw = jnp.dot(feats[side], proj[side], preferred_element_type=jnp.float32)
        inverse = lax.rsqrt(jnp.sum(raw * raw, axis=1, keepdims=True) + 1e-06)
        normal = raw * inverse
        unit[side] = normal
        recip[side] = inverse
        emb[side, 0] = normal.astype(jnp.bfloat16)
        if side == 0:
            pl.semaphore_wait(barrier, 3)
        for piece in range(CHUNKS):
            send(PARTNER, side, piece)
        for piece in range(CHUNKS):
            send(SIBLING, side, piece)

    def pull(side, row_slot, first, last):
        mine = emb[side, row_slot]
        theirs = emb[1 - side, first:last].reshape((last - first) * rows, mine.shape[1])
        logits = temper * lax.dot_general(
            mine, theirs, (((1,), (1,)), ((), ())), preferred_element_type=jnp.float32
        ) + offset
        slope = jax.nn.sigmoid(logits)
        if row_slot == 0 and first == 0:
            down = lax.broadcasted_iota(jnp.int32, slope.shape, 0)
            along = lax.broadcasted_iota(jnp.int32, slope.shape, 1)
            slope = slope - jnp.where(down == along, 1.0, 0.0)
        return jnp.dot(
            slope.astype(jnp.bfloat16), theirs, preferred_element_type=jnp.float32
        )

    for side in range(2):
        for piece in range(CHUNKS):
            copies[SIBLING, side, piece].wait_recv()
    for side in range(2):
        own_sum[side] = pull(side, 0, 0, 2)

    for piece in range(CHUNKS):
        for side in range(2):
            copies[PARTNER, side, piece].wait_recv()
            send(RELAY, side, piece)
    for side in (1, 0):
        away_sum[side] = pull(side, 2, 0, 3)

    for side in (1, 0):
        for piece in range(CHUNKS):
            copies[RELAY, 1 - side, piece].wait_recv()
        away_out[side] = (away_sum[side] + pull(side, 2, 3, 4)).astype(jnp.bfloat16)
        for piece in range(CHUNKS):
            send(BACK, side, piece)
    for side in (1, 0):
        own_sum[side] += pull(side, 0, 2, 4)

    outs = (image_grad, text_grad)
    for piece in range(CHUNKS):
        span = pl.ds(piece * part, part)
        for side in (1, 0):
            copies[BACK, side, piece].wait_recv()
            slope = temper * (own_sum[side, span] + away_in[side, span].astype(jnp.float32))
            normal = unit[side, span]
            inner = jnp.sum(normal * slope, axis=1, keepdims=True)
            down = (recip[side, span] * (slope - normal * inner)).astype(jnp.bfloat16)
            outs[side][span] = lax.dot_general(
                down, proj[side], (((1,), (1,)), ((), ())), preferred_element_type=jnp.float32
            )

    for copy in copies.values():
        copy.wait_send()


def on_device(axis_sizes, image_feats, text_feats, image_proj, text_proj, scale, bias):
    rows, width = image_feats.shape
    embed = image_proj.shape[1]
    out = jax.ShapeDtypeStruct((rows, width), jnp.float32)
    anywhere = pl.BlockSpec(memory_space=pl.ANY)
    scalar = pl.BlockSpec(memory_space=pltpu.SMEM)
    vmem = pl.BlockSpec(memory_space=pltpu.VMEM)
    return pl.pallas_call(
        functools.partial(kernel, axis_sizes),
        out_shape=(out, out),
        in_specs=[anywhere] * 4 + [scalar] * 2,
        out_specs=(vmem, vmem),
        scratch_shapes=[
            pltpu.VMEM((2, rows, width), jnp.bfloat16),
            pltpu.VMEM((2, width, embed), jnp.bfloat16),
            pltpu.VMEM((2, 4, rows, embed), jnp.bfloat16),
            pltpu.VMEM((2, rows, embed), jnp.float32),
            pltpu.VMEM((2, rows, 1), jnp.float32),
            pltpu.VMEM((2, rows, embed), jnp.float32),
            pltpu.VMEM((2, rows, embed), jnp.float32),
            pltpu.VMEM((2, rows, embed), jnp.bfloat16),
            pltpu.VMEM((2, rows, embed), jnp.bfloat16),
            pltpu.SemaphoreType.DMA((2, 2)),
            pltpu.SemaphoreType.DMA((4, 2, CHUNKS)),
            pltpu.SemaphoreType.DMA((4, 2, CHUNKS)),
        ],
        compiler_params=pltpu.CompilerParams(
            collective_id=0, has_side_effects=True, vmem_limit_bytes=48 * 1024 * 1024
        ),
    )(image_feats, text_feats, image_proj, text_proj, scale, bias)


def solution(mesh):
    in_specs = (P(("hst", "local"), None), P(("hst", "local"), None), P(), P(), P(), P())
    out_specs = (P(("hst", "local"), None), P(("hst", "local"), None))
    axis_sizes = (mesh.shape["hst"], mesh.shape["local"])
    return jax.shard_map(
        functools.partial(on_device, axis_sizes),
        mesh=mesh,
        in_specs=in_specs,
        out_specs=out_specs,
        check_vma=False,
    )
```

time: 72.9 us -> 32.2 us (0.44); the launches traced: 71.8 us -> 32 us
  matrix products: 50.2 us -> 0 us
  Pallas kernels: 0 us -> 24.7 us
  waiting for transfers between devices: 9.71 us -> 0 us
  starting transfers between devices: 9.06 us -> 0 us
  local copies, waits for them, and re-layouts: 0.62 us -> 5.3 us
    dot_general x21 -> x0, matrix products: 50.2 us -> none  [the longest x8 20 us: on_device(): jnp.dot(own_images, text_block, preferred_element_type=jnp.float32)]
    pallas_call x0 -> x1, Pallas kernels: none -> 24.7 us  [on_device(): pl.pallas_call(functools.partial(kernel, axis_sizes), out_shape=(out, out...]
    ppermute x14 -> x0, waiting for transfers between devices: 9.71 us -> none  [passed_along(): lax.ppermute(value, axis, [(i, (i + by) % count) for i in range(count)])]
    ppermute x14 -> x0, starting transfers between devices: 9.06 us -> none  [passed_along(): lax.ppermute(value, axis, [(i, (i + by) % count) for i in range(count)])]
    unnamed x10 -> x8, local copies, waits for them, and re-layouts: 0.62 us -> 5.3 us
  transfers between devices with their start and end apart: 14 -> 0, of which waited for: 6 -> 0; matrix products, arithmetic and copies ran while one was open for 57% -> 0% of each run, Pallas kernels for 0% -> 0%
where the time goes in v1:
time: 32.2 us; the launch traced here: 32 us
  Pallas kernels  24.7 us (77%)
  local copies, waits for them, and re-layouts  5.3 us (16%)
  between operations  1.94 us (6%)
    pallas_call x1, Pallas kernels, on_device(): pl.pallas_call(functools.partial(kernel, axis_sizes), out_shape=(out, out...  24.7 us
    unnamed x8, local copies, waits for them, and re-layouts  5.3 us

profile of v1, /device:TPU:0, one launch (start us, length us, event | category | flops | bytes accessed | tf_op | source)
XLA Modules:
  0.0 32.0 jit_solution(9809861882574319688)
XLA Ops:
  1.9 0.0 copy-start
  1.9 1.7 %copy-done = bf16[1152,1152]{1,0:T(8,128)(2,1)S(1)} copy-done((bf16[1152,1152]{1,0:T(8,128)(2,1)S(1)}, bf16[1152,1152]{1,0:T(8,128)(2,1)}, u32[]{:S(2)}) %copy-start) | copy-done | bytes 2654232
  3.7 0.0 copy-start.1
  3.7 1.0 %copy-done.1 = bf16[128,1152]{1,0:T(8,128)(2,1)S(1)} copy-done((bf16[128,1152]{1,0:T(8,128)(2,1)S(1)}, bf16[128,1152]{1,0:T(8,128)(2,1)}, u32[]{:S(2)}) %copy-start.1) | copy-done | bytes 294936
  4.6 0.0 copy-start.2
  4.6 1.0 %copy-done.2 = bf16[128,1152]{1,0:T(8,128)(2,1)S(1)} copy-done((bf16[128,1152]{1,0:T(8,128)(2,1)S(1)}, bf16[128,1152]{1,0:T(8,128)(2,1)}, u32[]{:S(2)}) %copy-start.2) | copy-done | bytes 294936
  5.6 24.7 %shard_map.77 = (f32[128,1152]{1,0:T(8,128)S(1)}, f32[128,1152]{1,0:T(8,128)S(1)}) custom-call(bf16[128,1152]{1,0:T(8,128)(2,1)S(1)} %copy-done.1, bf16[128,1152]{1,0:T(8,128)(2,1)S(1)} %copy-done.2, bf16[1152,1152]{1,0:T(8,128)(2,1)S(1)} %copy-done, bf16[1152,1152]{1,0:T(8,128)(2,1)} %text_proj.1, f32[1]{0:T(128)S(6)} %copy.10.scale, f32[1]{0:T(128)S(6)} %copy.11.bias), custom_call_target="tpu_custom_call" | custom-call | tf_op jit(solution)/shard_map/pallas_call | solution.py:183
  30.3 0.8 %copy.12 = f32[128,1152]{1,0:T(8,128)} copy(f32[128,1152]{1,0:T(8,128)S(1)} %get-tuple-element.4) | data formatting | bytes 1179648
  31.2 0.8 %copy.13 = f32[128,1152]{1,0:T(8,128)} copy(f32[128,1152]{1,0:T(8,128)S(1)} %get-tuple-element.5) | data formatting | bytes 1179648
Async XLA Ops:
  1.9 1.8 %copy-start = (bf16[1152,1152]{1,0:T(8,128)(2,1)S(1)}, bf16[1152,1152]{1,0:T(8,128)(2,1)}, u32[]{:S(2)}) copy-start(bf16[1152,1152]{1,0:T(8,128)(2,1)} %image_proj.1) | copy-start | bytes 7962628
  3.7 1.0 %copy-start.1 = (bf16[128,1152]{1,0:T(8,128)(2,1)S(1)}, bf16[128,1152]{1,0:T(8,128)(2,1)}, u32[]{:S(2)}) copy-start(bf16[128,1152]{1,0:T(8,128)(2,1)} %image_feats.1) | copy-start | bytes 884740
  4.6 1.0 %copy-start.2 = (bf16[128,1152]{1,0:T(8,128)(2,1)S(1)}, bf16[128,1152]{1,0:T(8,128)(2,1)}, u32[]{:S(2)}) copy-start(bf16[128,1152]{1,0:T(8,128)(2,1)} %text_feats.1) | copy-start | bytes 884740

commit v2 on v1

--- a/solution.py
+++ b/solution.py
@@ -9,6 +9,7 @@
 
 GROUP_DEVS = 8
 CHUNKS = 2
+BACK_CHUNKS = 2
 SIBLING, PARTNER, RELAY, BACK = range(4)
 
 
@@ -22,12 +23,13 @@
     text_feats,
     image_proj,
     text_proj,
-    scale,
-    bias,
+    knobs,
     image_grad,
     text_grad,
     feats,
+    away_feats,
     proj,
+    proj_t,
     emb,
     unit,
     recip,
@@ -54,9 +56,6 @@
 
     rows = image_feats.shape[0]
     part = rows // CHUNKS
-    temper = scale[0]
-    offset = bias[0]
-
     feat_loads = []
     proj_loads = []
     for side, (feat_ref, proj_ref) in enumerate(
@@ -88,13 +87,15 @@
         )
 
     copies = {}
+    given = (image_feats, text_feats)
 
     def send(kind, side, piece):
-        span = pl.ds(piece * part, part)
+        size = rows // (BACK_CHUNKS if kind == BACK else CHUNKS)
+        span = pl.ds(piece * size, size)
         if kind == SIBLING:
             src, dst, device = emb.at[side, 0, span], emb.at[side, 1, span], sibling
         elif kind == PARTNER:
-            src, dst, device = emb.at[side, 0, span], emb.at[side, 2, span], partners[side]
+            src, dst, device = given[side].at[span], away_feats.at[side, span], partners[side]
         elif kind == RELAY:
             src, dst, device = emb.at[side, 2, span], emb.at[side, 3, span], sibling
         else:
@@ -103,24 +104,31 @@
         copy.start()
         copies[kind, side, piece] = copy
 
+    pl.semaphore_wait(barrier, 3)
+    for piece in range(CHUNKS):
+        for side in range(2):
+            send(PARTNER, side, piece)
+
+    def embed(rows_in, side):
+        raw = jnp.dot(rows_in, proj[side], preferred_element_type=jnp.float32)
+        inverse = lax.rsqrt(jnp.sum(raw * raw, axis=1, keepdims=True) + 1e-06)
+        return raw * inverse, inverse
+
     for side in range(2):
         feat_loads[side].wait()
         proj_loads[side].wait()
-        raw = jnp.dot(feats[side], proj[side], preferred_element_type=jnp.float32)
-        inverse = lax.rsqrt(jnp.sum(raw * raw, axis=1, keepdims=True) + 1e-06)
-        normal = raw * inverse
+        normal, inverse = embed(feats[side], side)
         unit[side] = normal
         recip[side] = inverse
         emb[side, 0] = normal.astype(jnp.bfloat16)
-        if side == 0:
-            pl.semaphore_wait(barrier, 3)
-        for piece in range(CHUNKS):
-            send(PARTNER, side, piece)
         for piece in range(CHUNKS):
             send(SIBLING, side, piece)
 
-    def pull(side, row_slot, first, last):
-        mine = emb[side, row_slot]
+    temper = knobs[0:1, 0:1]
+    offset = knobs[1:2, 0:1]
+
+    def pull(side, row_slot, span, first, last):
+        mine = emb[side, row_slot, span]
         theirs = emb[1 - side, first:last].reshape((last - first) * rows, mine.shape[1])
         logits = temper * lax.dot_general(
             mine, theirs, (((1,), (1,)), ((), ())), preferred_element_type=jnp.float32
@@ -134,30 +142,39 @@
             slope.astype(jnp.bfloat16), theirs, preferred_element_type=jnp.float32
         )
 
+    whole = pl.ds(0, rows)
     for side in range(2):
         for piece in range(CHUNKS):
             copies[SIBLING, side, piece].wait_recv()
     for side in range(2):
-        own_sum[side] = pull(side, 0, 0, 2)
+        own_sum[side] = pull(side, 0, whole, 0, 2)
 
     for piece in range(CHUNKS):
+        span = pl.ds(piece * part, part)
         for side in range(2):
             copies[PARTNER, side, piece].wait_recv()
+            emb[side, 2, span] = embed(away_feats[side, span], side)[0].astype(jnp.bfloat16)
             send(RELAY, side, piece)
+        for side in (1, 0):
+            away_sum[side, span] = pull(side, 2, span, 0, 2)
+        if piece == 0:
+            for side in range(2):
+                proj_t[side] = proj[side].T
     for side in (1, 0):
-        away_sum[side] = pull(side, 2, 0, 3)
+        away_sum[side] += pull(side, 2, whole, 2, 3)
 
     for side in (1, 0):
         for piece in range(CHUNKS):
             copies[RELAY, 1 - side, piece].wait_recv()
-        away_out[side] = (away_sum[side] + pull(side, 2, 3, 4)).astype(jnp.bfloat16)
-        for piece in range(CHUNKS):
+        away_out[side] = (away_sum[side] + pull(side, 2, whole, 3, 4)).astype(jnp.bfloat16)
+        for piece in range(BACK_CHUNKS):
             send(BACK, side, piece)
     for side in (1, 0):
-        own_sum[side] += pull(side, 0, 2, 4)
+        own_sum[side] += pull(side, 0, whole, 2, 4)
 
     outs = (image_grad, text_grad)
-    for piece in range(CHUNKS):
+    part = rows // BACK_CHUNKS
+    for piece in range(BACK_CHUNKS):
         span = pl.ds(piece * part, part)
         for side in (1, 0):
             copies[BACK, side, piece].wait_recv()
@@ -165,8 +182,8 @@
             normal = unit[side, span]
             inner = jnp.sum(normal * slope, axis=1, keepdims=True)
             down = (recip[side, span] * (slope - normal * inner)).astype(jnp.bfloat16)
-            outs[side][span] = lax.dot_general(
-                down, proj[side], (((1,), (1,)), ((), ())), preferred_element_type=jnp.float32
+            outs[side][span] = jnp.dot(
+                down, proj_t[side], preferred_element_type=jnp.float32
             )
 
     for copy in copies.values():
@@ -177,17 +194,18 @@
     rows, width = image_feats.shape
     embed = image_proj.shape[1]
     out = jax.ShapeDtypeStruct((rows, width), jnp.float32)
-    anywhere = pl.BlockSpec(memory_space=pl.ANY)
-    scalar = pl.BlockSpec(memory_space=pltpu.SMEM)
+    anywhere = pl.BlockSpec(memory_space=pltpu.HBM)
     vmem = pl.BlockSpec(memory_space=pltpu.VMEM)
     return pl.pallas_call(
         functools.partial(kernel, axis_sizes),
         out_shape=(out, out),
-        in_specs=[anywhere] * 4 + [scalar] * 2,
+        in_specs=[anywhere] * 4 + [vmem],
         out_specs=(vmem, vmem),
         scratch_shapes=[
             pltpu.VMEM((2, rows, width), jnp.bfloat16),
+            pltpu.VMEM((2, rows, width), jnp.bfloat16),
             pltpu.VMEM((2, width, embed), jnp.bfloat16),
+            pltpu.VMEM((2, embed, width), jnp.bfloat16),
             pltpu.VMEM((2, 4, rows, embed), jnp.bfloat16),
             pltpu.VMEM((2, rows, embed), jnp.float32),
             pltpu.VMEM((2, rows, 1), jnp.float32),
@@ -196,13 +214,15 @@
             pltpu.VMEM((2, rows, embed), jnp.bfloat16),
             pltpu.VMEM((2, rows, embed), jnp.bfloat16),
             pltpu.SemaphoreType.DMA((2, 2)),
-            pltpu.SemaphoreType.DMA((4, 2, CHUNKS)),
-            pltpu.SemaphoreType.DMA((4, 2, CHUNKS)),
+            pltpu.SemaphoreType.DMA((4, 2, max(CHUNKS, BACK_CHUNKS))),
+            pltpu.SemaphoreType.DMA((4, 2, max(CHUNKS, BACK_CHUNKS))),
         ],
         compiler_params=pltpu.CompilerParams(
-            collective_id=0, has_side_effects=True, vmem_limit_bytes=48 * 1024 * 1024
+            collective_id=0, has_side_effects=True, vmem_limit_bytes=52428800
         ),
-    )(image_feats, text_feats, image_proj, text_proj, scale, bias)
+    )(
+        *(pltpu.with_memory_space_constraint(x, pltpu.HBM) for x in (image_feats, text_feats, image_proj, text_proj)), jnp.broadcast_to(jnp.stack([scale, bias]), (2, 128))
+    )
 
 
 def solution(mesh):

time: 32.2 us -> 28.8 us (0.89)
  local copies, waits for them, and re-layouts: 5.3 us -> 1.7 us
    unnamed x8 -> x2, local copies, waits for them, and re-layouts: 5.3 us -> 1.63 us
where the time goes in v2:
time: 28.8 us; the launch traced here: 28.6 us
  Pallas kernels  24.9 us (86%)
  between operations  1.93 us (7%)
  local copies, waits for them, and re-layouts  1.7 us (6%)
    pallas_call x1, Pallas kernels, on_device(): pl.pallas_call(functools.partial(kernel, axis_sizes), out_shape=(out, out...  24.9 us
    unnamed x2, local copies, waits for them, and re-layouts  1.63 us

profile of v2, /device:TPU:0, one launch (start us, length us, event | category | flops | bytes accessed | tf_op | source)
XLA Modules:
  0.0 28.6 jit_solution(17368702045625220972)
XLA Ops:
  1.9 0.1 maximum_bitcast_fusion
  2.0 0.1 broadcast_in_dim.8.knobs
  2.1 24.9 %shard_map.77 = (f32[128,1152]{1,0:T(8,128)S(1)}, f32[128,1152]{1,0:T(8,128)S(1)}) custom-call(bf16[128,1152]{1,0:T(8,128)(2,1)} %image_feats.1, bf16[128,1152]{1,0:T(8,128)(2,1)} %text_feats.1, bf16[1152,1152]{1,0:T(8,128)(2,1)} %image_proj.1, bf16[1152,1152]{1,0:T(8,128)(2,1)} %text_proj.1, f32[2,128]{1,0:T(2,128)S(1)} %broadcast_in_dim.8.knobs), custom_call_target="tpu_custom_call" | custom-call | tf_op jit(solution)/shard_map/pallas_call | solution.py:199
  27.0 0.8 %copy.12 = f32[128,1152]{1,0:T(8,128)} copy(f32[128,1152]{1,0:T(8,128)S(1)} %get-tuple-element.4) | data formatting | bytes 1179648
  27.8 0.8 %copy.13 = f32[128,1152]{1,0:T(8,128)} copy(f32[128,1152]{1,0:T(8,128)S(1)} %get-tuple-element.5) | data formatting | bytes 1179648

commit v3 on v2

--- a/solution.py
+++ b/solution.py
@@ -157,9 +157,6 @@
             send(RELAY, side, piece)
         for side in (1, 0):
             away_sum[side, span] = pull(side, 2, span, 0, 2)
-        if piece == 0:
-            for side in range(2):
-                proj_t[side] = proj[side].T
     for side in (1, 0):
         away_sum[side] += pull(side, 2, whole, 2, 3)
 
@@ -171,6 +168,8 @@
             send(BACK, side, piece)
     for side in (1, 0):
         own_sum[side] += pull(side, 0, whole, 2, 4)
+    for side in (1, 0):
+        proj_t[side] = proj[side].T
 
     outs = (image_grad, text_grad)
     part = rows // BACK_CHUNKS

time: 28.8 us -> 28.6 us (level)
  no operation moved by 1% of the time
where the time goes in v3:
time: 28.6 us; the launch traced here: 28.4 us
  Pallas kernels  24.7 us (86%)
  between operations  1.93 us (7%)
  local copies, waits for them, and re-layouts  1.7 us (6%)
    pallas_call x1, Pallas kernels, on_device(): pl.pallas_call(functools.partial(kernel, axis_sizes), out_shape=(out, out...  24.7 us
    unnamed x2, local copies, waits for them, and re-layouts  1.63 us

profile of v3, /device:TPU:0, one launch (start us, length us, event | category | flops | bytes accessed | tf_op | source)
XLA Modules:
  0.0 28.4 jit_solution(5596951025211898507)
XLA Ops:
  1.9 0.1 maximum_bitcast_fusion
  2.0 0.1 broadcast_in_dim.8.knobs
  2.1 24.7 %shard_map.77 = (f32[128,1152]{1,0:T(8,128)S(1)}, f32[128,1152]{1,0:T(8,128)S(1)}) custom-call(bf16[128,1152]{1,0:T(8,128)(2,1)} %image_feats.1, bf16[128,1152]{1,0:T(8,128)(2,1)} %text_feats.1, bf16[1152,1152]{1,0:T(8,128)(2,1)} %image_proj.1, bf16[1152,1152]{1,0:T(8,128)(2,1)} %text_proj.1, f32[2,128]{1,0:T(2,128)S(1)} %broadcast_in_dim.8.knobs), custom_call_target="tpu_custom_call" | custom-call | tf_op jit(solution)/shard_map/pallas_call | solution.py:198
  26.8 0.8 %copy.12 = f32[128,1152]{1,0:T(8,128)} copy(f32[128,1152]{1,0:T(8,128)S(1)} %get-tuple-element.4) | data formatting | bytes 1179648
  27.6 0.8 %copy.13 = f32[128,1152]{1,0:T(8,128)} copy(f32[128,1152]{1,0:T(8,128)S(1)} %get-tuple-element.5) | data formatting | bytes 1179648
